TPU v7x, 256 devices: a whole 4x4x8 slice. The times are simulated.
256 devices in a mesh: seq: 128 (over y, x_lo, z, core), mp: 2 (over x_hi).
Axes of the slice: x: 4 (x_hi: 2, x_lo: 2; x = x_hi * 2 + x_lo), y: 4, z: 8, core: 2. Of those that a mesh axis runs over, the one named last changes fastest.
Arguments:
- normed: bfloat16 [65536, 2048], P('seq', 'mp'), may hold values from -18 to 18
- router: bfloat16 [2048], replicated, may hold values from -0.125 to 0.125
- light_qkv: bfloat16 [3, 2048, 1024], P(None, None, 'mp'), may hold values from -0.125 to 0.125
- light_out: bfloat16 [1024, 2048], P('mp'), may hold values from -0.1875 to 0.1875
- heavy_qkv: bfloat16 [3, 2048, 1024], P(None, 'seq', 'mp'), may hold values from -0.125 to 0.125
- heavy_out: bfloat16 [1024, 2048], P('mp', 'seq'), may hold values from -0.1875 to 0.1875
- query_slots: int32 [128, 32], P('seq'), may hold values from 0 to 511, as said below
- query_count: int32 [128], P('seq'), may hold values from 1 to 32, 2048 in all
- key_slots: int32 [128, 32], P('seq'), may hold values from 0 to 511, as said below
- key_count: int32 [128], P('seq'), may hold values from 1 to 32, 2048 in all
Outputs:
- mixed: bfloat16 [65536, 2048], P('seq', 'mp')
Inputs may be any that keep to these rules, and one draw needn't show every extreme that they name: `query_slots`: each row holds 32 distinct positions of one shard's 512 tokens; only the first query_count entries of a row are live. `key_slots`: each row holds 32 distinct positions of one shard's 512 tokens; only the first key_count entries of a row are live. `query_count`: the counts sum to 2048 and the largest is exactly 32. `key_count`: the counts sum to 2048 and the largest is exactly 32.
All inputs are finite; a program needn't handle non-finite values.
Results may differ from a plain program's by a relative error of at most 0.012.
Values may be sent and summed in bfloat16 or wider, within the bound.
No kernel may reach another device: no remote copies, remote signals or barrier semaphores. Data moves between devices by JAX's collectives and lax.ppermute only.
A program may use at most 128 MiB of HBM per device.

v0:
```python
import jax
import jax.numpy as jnp
from jax import lax
from jax.sharding import PartitionSpec as P

HEAD_DIM = 64
RADIUS = 64
NEG = -1e30


def padded(cells, sides, width):
    for axis, dim in sides:
        count = lax.axis_size(axis)
        ends = count - 1
        head = lax.slice_in_dim(cells, 0, width, axis=dim)
        tail = lax.slice_in_dim(cells, cells.shape[dim] - width, cells.shape[dim], axis=dim)
        cells = jnp.concatenate(
            [
                lax.ppermute(tail, axis, [(i, (i + 1) % count) for i in range(ends)]),
                cells,
                lax.ppermute(head, axis, [((i + 1) % count, i) for i in range(ends)]),
            ],
            axis=dim,
        )
    return cells


def mix_heads(queries, key_rows, value_rows, allowed):
    length = queries.shape[0]
    head_count = queries.shape[1] // HEAD_DIM
    query_heads = queries.reshape(length, head_count, HEAD_DIM)
    key_heads = key_rows.reshape(key_rows.shape[0], head_count, HEAD_DIM)
    value_heads = value_rows.reshape(value_rows.shape[0], head_count, HEAD_DIM)
    scores = jnp.einsum(
        "qhe,khe->hqk", query_heads, key_heads, preferred_element_type=jnp.float32
    ) * HEAD_DIM ** (-0.5)
    scores = jnp.where(allowed[None], scores, NEG)
    row_peak = jnp.max(scores, axis=2, keepdims=True)
    weights = jnp.where(allowed[None], jnp.exp(scores - row_peak), 0.0)
    row_total = jnp.sum(weights, axis=2)
    blended = jnp.einsum(
        "hqk,khe->qhe",
        weights.astype(jnp.bfloat16),
        value_heads,
        preferred_element_type=jnp.float32,
    )
    blended = blended / jnp.transpose(row_total)[:, :, None]
    return blended.reshape(length, head_count * HEAD_DIM).astype(jnp.bfloat16)


def shards(
    normed,
    router,
    light_qkv,
    light_out,
    heavy_qkv,
    heavy_out,
    query_slots,
    query_count,
    key_slots,
    key_count,
):
    local_rows = normed.shape[0]
    shard_index = lax.axis_index("seq")
    shard_total = lax.axis_size("seq")
    capacity = query_slots.shape[1]
    features = lax.all_gather(normed, "mp", axis=1, tiled=True)
    queries = jnp.dot(features, light_qkv[0], preferred_element_type=jnp.float32).astype(
        jnp.bfloat16
    )
    paired = jnp.einsum(
        "td,cdh->cth", features, light_qkv[1:], preferred_element_type=jnp.float32
    ).astype(jnp.bfloat16)
    paired = padded(paired, (("seq", 1),), RADIUS)
    key_rows = paired[0]
    value_rows = paired[1]
    block_rows = min(512, local_rows)
    first_row = shard_index * local_rows
    query_pos = first_row + 0 + jnp.arange(block_rows, dtype=jnp.int32)
    key_pos = first_row + 0 - RADIUS + jnp.arange(block_rows + 2 * RADIUS, dtype=jnp.int32)
    distance = jnp.abs(query_pos[:, None] - key_pos[None, :])
    allowed = (
        (distance <= RADIUS)
        & (key_pos[None, :] >= 0)
        & (key_pos[None, :] < local_rows * shard_total)
    )
    outputs = mix_heads(queries, key_rows, value_rows, allowed)
    light_part = jnp.dot(outputs, light_out, preferred_element_type=jnp.float32)
    slot_range = jnp.arange(capacity, dtype=jnp.int32)
    query_live = slot_range < query_count[0]
    key_live = (slot_range < key_count[0]).astype(jnp.bfloat16)
    query_inputs = features[query_slots[0]]
    key_inputs = features[key_slots[0]]
    portion = lax.all_gather(heavy_qkv, "seq", axis=1, tiled=True)
    heavy_query = jnp.dot(query_inputs, portion[0], preferred_element_type=jnp.float32)
    heavy_key = jnp.dot(key_inputs, portion[1], preferred_element_type=jnp.float32)
    heavy_value = jnp.dot(key_inputs, portion[2], preferred_element_type=jnp.float32)
    heavy_query = heavy_query.astype(jnp.bfloat16)
    heavy_key = heavy_key.astype(jnp.bfloat16)
    heavy_value = heavy_value.astype(jnp.bfloat16)
    head_count = heavy_query.shape[1] // HEAD_DIM
    scale = HEAD_DIM ** (-0.5)
    query_heads = heavy_query.reshape(capacity, head_count, HEAD_DIM)
    row_peak = jnp.full((capacity, head_count), NEG, jnp.float32)
    key_part = lax.all_gather(heavy_key, "seq", axis=0, tiled=True)
    value_part = lax.all_gather(heavy_value, "seq", axis=0, tiled=True)
    live_part = lax.all_gather(key_live, "seq", axis=0, tiled=True)
    length = key_part.shape[0]
    key_heads = key_part.reshape(length, head_count, HEAD_DIM)
    value_heads = value_part.reshape(length, head_count, HEAD_DIM)
    live = live_part[None, None, :] > 0
    scores = (
        jnp.einsum("qhe,khe->qhk", query_heads, key_heads, preferred_element_type=jnp.float32)
        * scale
    )
    scores = jnp.where(live, scores, NEG)
    new_peak = jnp.maximum(row_peak, jnp.max(scores, axis=2))
    weights = jnp.where(live, jnp.exp(scores - new_peak[:, :, None]), 0.0)
    row_total = jnp.sum(weights, axis=2)
    blended = jnp.einsum(
        "qhk,khe->qhe",
        weights.astype(jnp.bfloat16),
        value_heads,
        preferred_element_type=jnp.float32,
    )
    row_peak, row_total, blended = (new_peak, row_total, blended)
    blended = blended / row_total[:, :, None]
    heavy_context = blended.reshape(capacity, head_count * HEAD_DIM).astype(jnp.bfloat16)
    gate = jax.nn.sigmoid(jnp.dot(query_inputs, router, preferred_element_type=jnp.float32))
    gate = jnp.where(query_live, gate, 0.0)
    heavy_rows = (
        jnp.dot(
            heavy_context,
            lax.all_gather(heavy_out, "seq", axis=1, tiled=True),
            preferred_element_type=jnp.float32,
        )
        * gate[:, None]
    )
    combined = light_part.at[query_slots[0]].add(heavy_rows)
    return lax.psum_scatter(combined, "mp", scatter_dimension=1, tiled=True).astype(jnp.bfloat16)


def solution(mesh):
    in_specs = (
        P("seq", "mp"),
        P(),
        P(None, None, "mp"),
        P("mp", None),
        P(None, "seq", "mp"),
        P("mp", "seq"),
        P("seq", None),
        P("seq"),
        P("seq", None),
        P("seq"),
    )
    out_specs = P("seq", "mp")
    return jax.shard_map(shards, mesh=mesh, in_specs=in_specs, out_specs=out_specs, check_vma=False)
```

profile of v0, /device:TPU:1, one launch (start us, length us, event | category | flops | bytes accessed | tf_op | source)
XLA Modules:
  0.0 995.2 jit_solution(5200214284138071772)
XLA Ops:
  6.6 0.7 all-gather.6.cloned.1.call-update
  7.3 0.7 all-gather.8.cloned.1.call-update
  8.7 43.7 %all-gather.6.cloned.1.call-done = bf16[512,2048]{1,0:T(8,128)(2,1)} async-done(((bf16[512,1024]{1,0:T(8,128)(2,1)}), bf16[512,2048]{1,0:T(8,128)(2,1)}) %all-gather.6.cloned.1.call-update) | async-done | bytes 2097168 | tf_op jit(solution)/shard_map/all_gather | solution.py:67
  52.5 2.6 gather_fusion
  55.1 215.8 %all-gather.8.cloned.1.call-done = bf16[3,2048,512]{2,1,0:T(8,128)(2,1)} async-done(((bf16[3,16,512]{2,1,0:T(8,128)(2,1)}), bf16[3,2048,512]{2,1,0:T(8,128)(2,1)}) %all-gather.8.cloned.1.call-update) | async-done | bytes 6291472 | tf_op jit(solution)/shard_map/all_gather | solution.py:94
  270.9 2.7 fusion.56
  273.6 2.7 fusion.54
  279.9 280.5 %all-reduce = bf16[4096]{0:T(1024)(128)(2,1)S(1)} all-reduce(bf16[4096]{0:T(1024)(128)(2,1)S(1)} %dynamic-update-slice), channel_id=1, replica_groups=mesh['seq'=128,'mp'=2] {'seq'}, use_global_device_ids=true, to_apply=%add | all-reduce | flops 4096 | bytes 16384
  560.4 1.2 fusion.42
  561.7 5.3 fusion.30
  567.0 0.7 fusion.77
  567.7 1.9 collective-permute-start
  569.6 3.9 collective-permute-start.1
  573.5 3.8 fusion.43
  577.3 2.6 gather_fusion.1
  580.3 1.1 copy.17
  581.7 8.4 fusion.78
  590.1 4.2 fusion.46
  594.3 3.3 fusion.80
  597.6 2.0 fusion.55
  599.8 6.7 copy.19
  606.5 96.9 %all-gather.10.cloned.1.call-done = bf16[4096,512]{1,0:T(8,128)(2,1)} async-done(((bf16[32,512]{1,0:T(8,128)(2,1)}), bf16[4096,512]{1,0:T(8,128)(2,1)}) %all-gather.10.cloned.1.call-update) | async-done | bytes 4194320 | tf_op jit(solution)/shard_map/all_gather | solution.py:106
  703.4 6.5 copy.18
  709.9 3.2 fusion.79
  713.0 0.9 fusion.11
  713.9 1.3 copy-done.1
  715.2 1.3 fusion.65
  716.7 201.3 %all-gather.14.cloned.1.call-done = bf16[512,2048]{0,1:T(8,128)(2,1)} async-done(((bf16[512,16]{0,1:T(8,128)(2,1)}), bf16[512,2048]{0,1:T(8,128)(2,1)}) %all-gather.14.cloned.1.call-update) | async-done | bytes 2097168 | tf_op jit(solution)/shard_map/all_gather | solution.py:134
  918.0 2.3 convolution_multiply_fusion.1
  920.4 5.1 scatter_fusion
  925.5 60.1 %reduce-scatter.2.cloned.1.call-done = f32[512,1024]{1,0:T(8,128)} async-done(((f32[512,2048]{1,0:T(8,128)}), f32[512,1024]{1,0:T(8,128)}) %reduce-scatter.2.cloned.1.call-update) | async-done | bytes 2097168 | tf_op jit(solution)/shard_map/reduce_scatter | solution.py:140
  985.6 2.7 convert_element_type.55
  (49 shorter events, 3.3 us)
Async XLA Ops:
  6.5 587.8 %copy-start = (bf16[512,2048]{1,0:T(8,128)(2,1)S(1)}, bf16[512,2048]{1,0:T(8,128)(2,1)}, u32[]{:S(2)}) copy-start(bf16[512,2048]{1,0:T(8,128)(2,1)} %param.13) | copy-start | bytes 6291460
  6.5 271.8 %copy-start.7 = (u32[256]{0:T(256)S(1)}, u32[256]{0:T(256)}, u32[]{:S(2)}) copy-start(u32[256]{0:T(256)} %constant.41) | copy-start | bytes 3076
  6.5 271.8 %copy-start.6 = (s32[1,32]{1,0:T(1,128)S(1)}, s32[1,32]{1,0:T(1,128)}, u32[]{:S(2)}) copy-start(s32[1,32]{1,0:T(1,128)} %param.16) | copy-start | bytes 388
  6.5 271.8 %copy-start.3 = (bf16[2048]{0:T(1024)(128)(2,1)S(1)}, bf16[2048]{0:T(1024)(128)(2,1)}, u32[]{:S(2)}) copy-start(bf16[2048]{0:T(1024)(128)(2,1)} %param.11) | copy-start | bytes 12292
  6.5 45.9 %all-gather.6.cloned.1.call-start = ((), (), s32[]{:S(2)}) async-start(), calls=%async_computation.1 | async-start | bytes 3145728 | tf_op jit(solution)/shard_map/all_gather | solution.py:67
  7.3 263.6 %all-gather.8.cloned.1.call-start = ((), (), s32[]{:S(2)}) async-start(), calls=%async_computation.2 | async-start | bytes 6340608 | tf_op jit(solution)/shard_map/all_gather | solution.py:94
  8.0 591.8 %all-gather.12.cloned.1.call-start = ((), (), s32[]{:S(2)}) async-start(), calls=%async_computation.4 | async-start | bytes 4227072 | tf_op jit(solution)/shard_map/all_gather | solution.py:105
  273.6 429.8 %all-gather.10.cloned.1.call-start = ((), (), s32[]{:S(2)}) async-start(), calls=%async_computation.3 | async-start | bytes 4227072 | tf_op jit(solution)/shard_map/all_gather | solution.py:106
  276.3 641.7 %all-gather.14.cloned.1.call-start = ((), (), s32[]{:S(2)}) async-start(), calls=%async_computation.5 | async-start | bytes 2113536 | tf_op jit(solution)/shard_map/all_gather | solution.py:134
  276.9 708.7 %reduce-scatter.2.cloned.1.call-start = ((), (), s32[]{:S(2)}) async-start(), calls=%async_computation.6 | async-start | bytes 6291456 | tf_op jit(solution)/shard_map/reduce_scatter | solution.py:140
  278.3 282.1 %copy-start.4 = (s32[32]{0:T(128)}, s32[32]{0:T(128)S(1)}, u32[]{:S(2)}) copy-start(s32[32]{0:T(128)S(1)} %fusion.71) | copy-start | bytes 388
  561.7 11.9 %copy-start.2 = (bf16[512,2048]{1,0:T(8,128)(2,1)S(1)}, bf16[512,2048]{1,0:T(8,128)(2,1)}, u32[]{:S(2)}) copy-start(bf16[512,2048]{1,0:T(8,128)(2,1)} %all-gather.6.cloned.1.call-done) | copy-start | bytes 6291460
  567.7 12.4 %collective-permute-start = (bf16[2,64,512]{2,1,0:T(8,128)(2,1)}, bf16[2,64,512]{2,1,0:T(8,128)(2,1)S(1)}, u32[]{:S(2)}, u32[]{:S(2)}) collective-permute-start(bf16[2,64,512]{2,1,0:T(8,128)(2,1)} %get-tuple-element.7), channel_id=1, source_target_pairs={{0,2},{2,4},{4,6},{6,8},{8,10},{10,12},{12,14},{14,16},{16,18},{18... | collective-permute-start | bytes 393224 | tf_op jit(solution)/shard_map/ppermute | solution.py:19
  569.6 10.5 %collective-permute-start.1 = (bf16[2,64,512]{2,1,0:T(8,128)(2,1)}, bf16[2,64,512]{2,1,0:T(8,128)(2,1)S(1)}, u32[]{:S(2)}, u32[]{:S(2)}) collective-permute-start(bf16[2,64,512]{2,1,0:T(8,128)(2,1)} %get-tuple-element.8), channel_id=1, source_target_pairs={{2,0},{4,2},{6,4},{8,6},{10,8},{12,10},{14,12},{16,14},{18,16},{20... | collective-permute-start | bytes 393224 | tf_op jit(solution)/shard_map/ppermute | solution.py:21
  713.0 2.2 copy-start.1
  715.2 205.1 %copy-start.5 = (s32[32]{0:T(128)S(1)}, s32[32]{0:T(128)}, u32[]{:S(2)}) copy-start(s32[32]{0:T(128)} %copy-done.4) | copy-start | bytes 388
Sparse Core Ops, SparseCore 0:
  9.1 43.2 all-gather.5
  54.4 216.4 all-gather.7
  273.7 213.8 all-gather.11
  489.3 214.0 all-gather.9
  705.1 212.8 all-gather.13
  925.6 59.9 reduce-scatter.1
where the time goes:
time: 996 us; the launch traced here: 995 us
  waiting for transfers between devices  620 us (62%)
  blocking collectives  281 us (28%)
  matrix products  39.3 us (4%)
  local copies, waits for them, and re-layouts  23 us (2%)
  between operations  15.7 us (2%)
  other arithmetic  10.8 us (1%)
    unnamed x1, blocking collectives  281 us
    all_gather x1, waiting for transfers between devices, shards(): portion = lax.all_gather(heavy_qkv, 'seq', axis=1, tiled=True)  216 us
    all_gather x1, waiting for transfers between devices, shards(): lax.all_gather(heavy_out, 'seq', axis=1, tiled=True)  201 us
    all_gather x1, waiting for transfers between devices, shards(): value_part = lax.all_gather(heavy_value, 'seq', axis=0, tiled=True)  96.9 us
    reduce_scatter x1, waiting for transfers between devices, shards(): lax.psum_scatter(combined, 'mp', scatter_dimension=1, tiled=True)  60.1 us
    all_gather x1, waiting for transfers between devices, shards(): features = lax.all_gather(normed, 'mp', axis=1, tiled=True)  43.7 us
  transfers between devices with their start and end apart: 8, of which 5 were waited for; matrix products, arithmetic and copies ran while one was open for 6% of the time, Pallas kernels for 0%

commit v1 on v0

--- a/solution.py
+++ b/solution.py
@@ -6,6 +6,11 @@
 HEAD_DIM = 64
 RADIUS = 64
 NEG = -1e30
+
+
+def all_by_exchange(x, axis, dim):
+    sent = jnp.stack([x] * lax.axis_size(axis))
+    return jnp.concatenate(lax.all_to_all(sent, axis, 0, 0), axis=dim)
 
 
 def padded(cells, sides, width):
@@ -130,9 +135,7 @@
     gate = jnp.where(query_live, gate, 0.0)
     heavy_rows = (
         jnp.dot(
-            heavy_context,
-            lax.all_gather(heavy_out, "seq", axis=1, tiled=True),
-            preferred_element_type=jnp.float32,
+            heavy_context, all_by_exchange(heavy_out, "seq", 1), preferred_element_type=jnp.float32
         )
         * gate[:, None]
     )

time: 996 us -> 800 us (0.80)
  waiting for transfers between devices: 620 us -> 374 us
  blocking collectives: 281 us -> 318 us
  starting transfers between devices: 6.05 us -> 16.1 us
    all_gather x1 -> x0, waiting for transfers between devices: 201 us -> none  [shards(): lax.all_gather(heavy_out, 'seq', axis=1, tiled=True)]
    all_gather x1, waiting for transfers between devices: 96.9 us -> 53.2 us  [shards(): value_part = lax.all_gather(heavy_value, 'seq', axis=0, tiled=True)]
    unnamed x1, blocking collectives: 281 us -> 318 us
    all_to_all x0 -> x1, starting transfers between devices: none -> 10.5 us  [all_by_exchange(): return jnp.concatenate(lax.all_to_all(sent, axis, 0, 0), axis=dim)]
  transfers between devices with their start and end apart: 8 -> 8, of which waited for: 5 -> 4; matrix products, arithmetic and copies ran while one was open for 6% -> 8% of each run, Pallas kernels for 0% -> 0%
where the time goes in v1:
time: 800 us; the launch traced here: 799 us
  waiting for transfers between devices  374 us (47%)
  blocking collectives  318 us (40%)
  matrix products  39.3 us (5%)
  local copies, waits for them, and re-layouts  25.2 us (3%)
  starting transfers between devices  16.1 us (2%)
  between operations  15.4 us (2%)
  other arithmetic  10.8 us (1%)
    unnamed x1, blocking collectives  318 us
    all_gather x1, waiting for transfers between devices, shards(): portion = lax.all_gather(heavy_qkv, 'seq', axis=1, tiled=True)  216 us
    reduce_scatter x1, waiting for transfers between devices, shards(): lax.psum_scatter(combined, 'mp', scatter_dimension=1, tiled=True)  60.2 us
    all_gather x1, waiting for transfers between devices, shards(): value_part = lax.all_gather(heavy_value, 'seq', axis=0, tiled=True)  53.2 us
    all_gather x1, waiting for transfers between devices, shards(): features = lax.all_gather(normed, 'mp', axis=1, tiled=True)  43.7 us
  transfers between devices with their start and end apart: 8, of which 4 were waited for; matrix products, arithmetic and copies ran while one was open for 8% of the time, Pallas kernels for 0%

profile of v1, /device:TPU:1, one launch (start us, length us, event | category | flops | bytes accessed | tf_op | source)
XLA Modules:
  0.0 798.9 jit_solution(1919865420346143979)
XLA Ops:
  6.5 0.7 all-gather.5.cloned.1.call-update
  8.7 43.7 %all-gather.5.cloned.1.call-done = bf16[512,2048]{1,0:T(8,128)(2,1)} async-done(((bf16[512,1024]{1,0:T(8,128)(2,1)}), bf16[512,2048]{1,0:T(8,128)(2,1)}) %all-gather.5.cloned.1.call-update) | async-done | bytes 2097168 | tf_op jit(solution)/shard_map/all_gather | solution.py:72
  52.5 2.6 gather_fusion
  55.1 215.8 %all-gather.7.cloned.1.call-done = bf16[3,2048,512]{2,1,0:T(8,128)(2,1)} async-done(((bf16[3,16,512]{2,1,0:T(8,128)(2,1)}), bf16[3,2048,512]{2,1,0:T(8,128)(2,1)}) %all-gather.7.cloned.1.call-update) | async-done | bytes 6291472 | tf_op jit(solution)/shard_map/all_gather | solution.py:99
  270.9 2.7 fusion.56
  273.7 2.7 fusion.54
  276.4 1.6 stack.2
  278.0 10.5 %all-to-all-start = ((bf16[128,512,16]{1,2,0:T(8,128)(2,1)}), bf16[128,512,16]{1,2,0:T(8,128)(2,1)}, u32[]{:S(2)}, u32[]{:S(2)}) async-start(bf16[128,512,16]{1,2,0:T(8,128)(2,1)} %stack.2), calls=%async_computation | async-start | bytes 4194304 | tf_op jit(solution)/shard_map/all_to_all | solution.py:13
  291.5 317.7 %all-reduce = bf16[4096]{0:T(1024)(128)(2,1)S(1)} all-reduce(bf16[4096]{0:T(1024)(128)(2,1)S(1)} %dynamic-update-slice), channel_id=1, replica_groups=mesh['seq'=128,'mp'=2] {'seq'}, use_global_device_ids=true, to_apply=%add | all-reduce | flops 4096 | bytes 16384
  609.8 1.3 fusion.42
  611.0 5.3 fusion.30
  616.3 0.7 fusion.77
  617.0 1.9 collective-permute-start
  619.0 3.6 collective-permute-start.1
  622.5 3.7 fusion.43
  626.2 2.6 gather_fusion.1
  629.2 1.1 copy.18
  630.6 8.4 %fusion.78 = (f32[8,512]{1,0:T(8,128)S(1)}, bf16[8,512,640]{2,1,0:T(8,128)(2,1)}) fusion(pred[512,640]{1,0:T(8,128)(4,1)} %fusion.42, bf16[512,8,64]{0,2,1:T(8,128)(2,1)} %bitcast.101, bf16[640,8,64]{0,2,1:T(8,128)(2,1)} %bitcast.98), kind=kOutput, calls=%fused_computation.77 | convolution fusion | flops 351273600 | bytes 6766592 | tf_op jit(solution)/shard_map/sub | solution.py:44
  639.1 4.2 fusion.46
  643.3 3.3 fusion.80
  646.6 2.0 fusion.55
  648.8 6.7 copy.20
  655.4 53.2 %all-gather.9.cloned.1.call-done = bf16[4096,512]{1,0:T(8,128)(2,1)} async-done(((bf16[32,512]{1,0:T(8,128)(2,1)}), bf16[4096,512]{1,0:T(8,128)(2,1)}) %all-gather.9.cloned.1.call-update) | async-done | bytes 4194320 | tf_op jit(solution)/shard_map/all_gather | solution.py:111
  708.6 6.5 copy.19
  715.1 3.2 fusion.79
  718.3 0.9 fusion.11
  719.2 1.3 copy-done.1
  720.5 1.3 fusion.65
  722.0 2.3 convolution_multiply_fusion.1
  724.3 5.1 scatter_fusion
  729.4 60.2 %reduce-scatter.2.cloned.1.call-done = f32[512,1024]{1,0:T(8,128)} async-done(((f32[512,2048]{1,0:T(8,128)}), f32[512,1024]{1,0:T(8,128)}) %reduce-scatter.2.cloned.1.call-update) | async-done | bytes 2097168 | tf_op jit(solution)/shard_map/reduce_scatter | solution.py:143
  789.7 2.7 convert_element_type.55
  (51 shorter events, 4.0 us)
Async XLA Ops:
  6.5 636.8 %copy-start = (bf16[512,2048]{1,0:T(8,128)(2,1)S(1)}, bf16[512,2048]{1,0:T(8,128)(2,1)}, u32[]{:S(2)}) copy-start(bf16[512,2048]{1,0:T(8,128)(2,1)} %param.13) | copy-start | bytes 6291460
  6.5 269.8 %copy-start.3 = (bf16[512,16]{0,1:T(8,128)(2,1)S(1)}, bf16[512,16]{0,1:T(8,128)(2,1)}, u32[]{:S(2)}) copy-start(bf16[512,16]{0,1:T(8,128)(2,1)} %param.15) | copy-start | bytes 49156
  6.5 45.9 %all-gather.5.cloned.1.call-start = ((), (), s32[]{:S(2)}) async-start(), calls=%async_computation.2 | async-start | bytes 3145728 | tf_op jit(solution)/shard_map/all_gather | solution.py:72
  7.3 263.6 %all-gather.7.cloned.1.call-start = ((), (), s32[]{:S(2)}) async-start(), calls=%async_computation.3 | async-start | bytes 6340608 | tf_op jit(solution)/shard_map/all_gather | solution.py:99
  8.0 640.8 %all-gather.11.cloned.1.call-start = ((), (), s32[]{:S(2)}) async-start(), calls=%async_computation.5 | async-start | bytes 4227072 | tf_op jit(solution)/shard_map/all_gather | solution.py:110
  273.6 16.3 %copy-start.4 = (bf16[2048]{0:T(1024)(128)(2,1)S(1)}, bf16[2048]{0:T(1024)(128)(2,1)}, u32[]{:S(2)}) copy-start(bf16[2048]{0:T(1024)(128)(2,1)} %param.11) | copy-start | bytes 12292
  273.6 16.3 %copy-start.8 = (u32[256]{0:T(256)S(1)}, u32[256]{0:T(256)}, u32[]{:S(2)}) copy-start(u32[256]{0:T(256)} %constant.41) | copy-start | bytes 3076
  273.6 335.7 %copy-start.7 = (s32[1,32]{1,0:T(1,128)S(1)}, s32[1,32]{1,0:T(1,128)}, u32[]{:S(2)}) copy-start(s32[1,32]{1,0:T(1,128)} %param.16) | copy-start | bytes 388
  273.6 435.0 %all-gather.9.cloned.1.call-start = ((), (), s32[]{:S(2)}) async-start(), calls=%async_computation.4 | async-start | bytes 4227072 | tf_op jit(solution)/shard_map/all_gather | solution.py:111
  278.0 444.0 %all-to-all-start = ((bf16[128,512,16]{1,2,0:T(8,128)(2,1)}), bf16[128,512,16]{1,2,0:T(8,128)(2,1)}, u32[]{:S(2)}, u32[]{:S(2)}) async-start(bf16[128,512,16]{1,2,0:T(8,128)(2,1)} %stack.2), calls=%async_computation | async-start | bytes 4194304 | tf_op jit(solution)/shard_map/all_to_all | solution.py:13
  288.5 501.2 %reduce-scatter.2.cloned.1.call-start = ((), (), s32[]{:S(2)}) async-start(), calls=%async_computation.6 | async-start | bytes 6291456 | tf_op jit(solution)/shard_map/reduce_scatter | solution.py:143
  609.3 0.5 copy-start.5
  611.0 11.5 %copy-start.2 = (bf16[512,2048]{1,0:T(8,128)(2,1)S(1)}, bf16[512,2048]{1,0:T(8,128)(2,1)}, u32[]{:S(2)}) copy-start(bf16[512,2048]{1,0:T(8,128)(2,1)} %all-gather.5.cloned.1.call-done) | copy-start | bytes 6291460
  617.0 12.0 %collective-permute-start = (bf16[2,64,512]{2,1,0:T(8,128)(2,1)}, bf16[2,64,512]{2,1,0:T(8,128)(2,1)S(1)}, u32[]{:S(2)}, u32[]{:S(2)}) collective-permute-start(bf16[2,64,512]{2,1,0:T(8,128)(2,1)} %get-tuple-element.7), channel_id=1, source_target_pairs={{0,2},{2,4},{4,6},{6,8},{8,10},{10,12},{12,14},{14,16},{16,18},{18... | collective-permute-start | bytes 393224 | tf_op jit(solution)/shard_map/ppermute | solution.py:24
  619.0 10.1 %collective-permute-start.1 = (bf16[2,64,512]{2,1,0:T(8,128)(2,1)}, bf16[2,64,512]{2,1,0:T(8,128)(2,1)S(1)}, u32[]{:S(2)}, u32[]{:S(2)}) collective-permute-start(bf16[2,64,512]{2,1,0:T(8,128)(2,1)} %get-tuple-element.8), channel_id=1, source_target_pairs={{2,0},{4,2},{6,4},{8,6},{10,8},{12,10},{14,12},{16,14},{18,16},{20... | collective-permute-start | bytes 393224 | tf_op jit(solution)/shard_map/ppermute | solution.py:26
  718.3 2.2 copy-start.1
  720.5 3.8 copy-start.6
Sparse Core Ops, SparseCore 0:
  9.1 43.2 all-gather.4
  54.3 216.4 all-gather.6
  273.7 218.5 all-gather.10
  494.0 214.5 all-gather.8
  729.6 60.0 reduce-scatter.1
